TPU v7x, 32 devices: a whole 2x2x4 slice. The times are simulated.
32 devices in a mesh: row: 4 (over y, x), col: 8 (over z, core).
Axes of the slice: x: 2, y: 2, z: 4, core: 2. Of those that a mesh axis runs over, the one named last changes fastest.
Arguments:
- queries: float32 [2, 192, 20480], P(None, 'col', 'row'), may hold values from -6 to 6
- precond: float32 [20480, 20480], P('row', 'col'), may hold values from -0.0390625 to 0.0390625
- column_gain: float32 [20480], P('col'), may hold values from 0.5 to 2
- store: bfloat16 [12288, 20480], P('row', 'col'), may hold values from -0.0390625 to 0.0390625
Outputs:
- scores: float32 [2, 192, 12288], P(None, 'col', 'row')
All inputs are finite; a program needn't handle non-finite values.
Results may differ from a plain program's by a relative error of at most 0.0029.
Values sent between devices are 32-bit elements; how exact they have to be, the bound alone decides.
No kernel may reach another device: no remote copies, remote signals or barrier semaphores. Data moves between devices by JAX's collectives and lax.ppermute only.
A program may use at most 128 MiB of HBM per device.

v0:
```python
import jax
import jax.numpy as jnp
from jax import lax
from jax.sharding import PartitionSpec as P


def score_block(lowered, store):
    return lax.dot_general(
        lowered, store, (((1,), (1,)), ((), ())), preferred_element_type=jnp.float32
    )


def local(queries, precond, column_gain, store):
    results = []
    for batch_index in range(queries.shape[0]):
        local_rows = queries[batch_index]
        partial_rows = jnp.dot(
            lax.all_gather(local_rows, "col", axis=0, tiled=True),
            precond,
            precision=lax.Precision.HIGHEST,
            preferred_element_type=jnp.float32,
        )
        summed = lax.psum(partial_rows, "row")
        lowered = (summed * column_gain[None, :]).astype(jnp.bfloat16)
        own_scores = lax.psum_scatter(
            score_block(lowered, store), "col", scatter_dimension=0, tiled=True
        )
        results.append(own_scores)
    return jnp.stack(results)


def solution(mesh):
    return jax.shard_map(
        local,
        mesh=mesh,
        in_specs=(P(None, "col", "row"), P("row", "col"), P("col"), P("row", "col")),
        out_specs=P(None, "col", "row"),
        check_vma=False,
    )
```

profile of v0, /device:TPU:0, one launch (start us, length us, event | category | flops | bytes accessed | tf_op | source)
XLA Modules:
  0.0 335.7 jit_solution(14430148058530714590)
XLA Ops:
  6.5 0.0 all-gather.5.cloned.1.call-start
  6.5 2.2 fusion.8
  8.7 0.0 all-gather.5.cloned.1.call-update
  8.8 0.0 all-gather.7.cloned.1.call-start
  8.8 0.7 all-gather.7.cloned.1.call-update
  9.5 0.0 all-reduce.3.cloned.1.call-start
  9.6 46.9 %all-gather.5.cloned.1.call-done = f32[1,192,5120]{2,1,0:T(8,128)} async-done(((f32[1,24,5120]{2,1,0:T(8,128)}), f32[1,192,5120]{2,1,0:T(8,128)}) %all-gather.5.cloned.1.call-update) | async-done | bytes 3932176 | tf_op jit(solution)/shard_map/all_gather | solution.py:18
  56.4 38.3 %fusion.2 = f32[192,2560]{1,0:T(8,128)} fusion(f32[5120,2560]{1,0:T(8,128)} %param.5, f32[1,192,5120]{2,1,0:T(8,128)} %all-gather.5.cloned.1.call-done), kind=kOutput, calls=%fused_computation.2 | convolution fusion | flops 30198988800 | bytes 58327040 | tf_op jit(solution)/shard_map/dot_general | solution.py:17
  94.7 7.0 %all-gather.7.cloned.1.call-done = f32[1,192,5120]{2,1,0:T(8,128)} async-done(((f32[1,24,5120]{2,1,0:T(8,128)}), f32[1,192,5120]{2,1,0:T(8,128)}) %all-gather.7.cloned.1.call-update) | async-done | bytes 3932176 | tf_op jit(solution)/shard_map/all_gather | solution.py:18
  101.7 38.3 %fusion = f32[192,2560]{1,0:T(8,128)} fusion(f32[5120,2560]{1,0:T(8,128)} %param.5, f32[1,192,5120]{2,1,0:T(8,128)} %all-gather.7.cloned.1.call-done), kind=kOutput, calls=%fused_computation | convolution fusion | flops 30198988800 | bytes 58327040 | tf_op jit(solution)/shard_map/dot_general | solution.py:17
  140.0 0.0 copy-start.1
  140.0 0.0 all-reduce.3.cloned.1.call-update
  140.0 0.0 reduce-scatter.5.cloned.1.call-start
  140.1 99.0 %all-reduce.3.cloned.1.call-done = (f32[192,2560]{1,0:T(8,128)}, f32[192,2560]{1,0:T(8,128)}) async-done(((f32[192,2560]{1,0:T(8,128)}, f32[192,2560]{1,0:T(8,128)}), (f32[192,2560]{1,0:T(8,128)}, f32[192,2560]{1,0:T(8,128)})) %all-reduce.3.cloned.1.call-update) | async-done | bytes 3932176 | tf_op jit(solution)/shard_map/psum | solution.py:23
  239.0 0.0 copy-done.1
  239.0 0.0 copy-start
  239.0 12.8 %fusion.5 = f32[192,3072]{1,0:T(8,128)} fusion(bf16[3072,2560]{1,0:T(8,128)(2,1)} %param.7, f32[192,2560]{1,0:T(8,128)} %get-tuple-element.5, f32[2560]{0:T(1024)S(1)} %copy-done.1), kind=kOutput, calls=%fused_computation.7 | convolution fusion | flops 3020881920 | bytes 20064256 | tf_op jit(solution)/shard_map/dot_general | solution.py:8
  251.9 0.0 reduce-scatter.5.cloned.1.call-update
  251.9 0.2 reduce-scatter.3.cloned.1.call-start
  252.1 0.0 copy-done
  252.2 12.1 %fusion.4 = f32[192,3072]{1,0:T(8,128)} fusion(bf16[3072,2560]{1,0:T(8,128)(2,1)} %param.7, f32[192,2560]{1,0:T(8,128)S(1)} %copy-done, f32[2560]{0:T(1024)S(1)} %copy-done.1), kind=kOutput, calls=%fused_computation.6 | convolution fusion | flops 3020881920 | bytes 20064256 | tf_op jit(solution)/shard_map/dot_general | solution.py:8
  264.3 0.0 reduce-scatter.3.cloned.1.call-update
  264.3 24.8 %reduce-scatter.5.cloned.1.call-done = f32[24,3072]{1,0:T(8,128)} async-done(((f32[192,3072]{1,0:T(8,128)}), f32[24,3072]{1,0:T(8,128)}) %reduce-scatter.5.cloned.1.call-update) | async-done | bytes 294928 | tf_op jit(solution)/shard_map/reduce_scatter | solution.py:25
  289.1 38.2 %reduce-scatter.3.cloned.1.call-done = f32[24,3072]{1,0:T(8,128)} async-done(((f32[192,3072]{1,0:T(8,128)}), f32[24,3072]{1,0:T(8,128)}) %reduce-scatter.3.cloned.1.call-update) | async-done | bytes 294928 | tf_op jit(solution)/shard_map/reduce_scatter | solution.py:25
  327.3 1.9 pad_maximum_fusion
Async XLA Ops:
  6.5 49.9 %all-gather.5.cloned.1.call-start = ((), (), s32[]{:S(2)}) async-start(), calls=%async_computation.4 | async-start | bytes 4423680 | tf_op jit(solution)/shard_map/all_gather | solution.py:18
  8.8 92.9 %all-gather.7.cloned.1.call-start = ((), (), s32[]{:S(2)}) async-start(), calls=%async_computation.5 | async-start | bytes 4423680 | tf_op jit(solution)/shard_map/all_gather | solution.py:18
  9.5 229.5 %all-reduce.3.cloned.1.call-start = ((), (), s32[]{:S(2)}) async-start(), calls=%async_computation.6 | async-start | bytes 7864320 | tf_op jit(solution)/shard_map/psum | solution.py:23
  140.0 99.1 %copy-start.1 = (f32[2560]{0:T(1024)S(1)}, f32[2560]{0:T(1024)}, u32[]{:S(2)}) copy-start(f32[2560]{0:T(1024)} %param.6) | copy-start | bytes 30724
  140.0 149.1 %reduce-scatter.5.cloned.1.call-start = ((), (), s32[]{:S(2)}) async-start(), calls=%async_computation.3 | async-start | bytes 2654208 | tf_op jit(solution)/shard_map/reduce_scatter | solution.py:25
  239.0 13.1 %copy-start = (f32[192,2560]{1,0:T(8,128)S(1)}, f32[192,2560]{1,0:T(8,128)}, u32[]{:S(2)}) copy-start(f32[192,2560]{1,0:T(8,128)} %get-tuple-element.6) | copy-start | bytes 5898244
  251.9 75.4 %reduce-scatter.3.cloned.1.call-start = ((), (), s32[]{:S(2)}) async-start(), calls=%async_computation.2 | async-start | bytes 2654208 | tf_op jit(solution)/shard_map/reduce_scatter | solution.py:25
Sparse Core Ops, SparseCore 0:
  9.0 47.4 all-gather.4
  58.1 43.5 all-gather.6
  140.1 98.8 all-reduce.2
  252.0 37.0 reduce-scatter.4
  291.3 35.9 reduce-scatter.2
where the time goes:
time: 336 us
  waiting for transfers between devices  217 us (65%)
  matrix products  102 us (30%)
  between operations  13.2 us (4%)
    psum x1, waiting for transfers between devices, local(): summed = lax.psum(partial_rows, 'row')  99 us
    dot_general x2, matrix products, local(): jnp.dot(lax.all_gather(local_rows, 'col', axis=0, tiled=True), precond, p...  76.6 us
    reduce_scatter x2, waiting for transfers between devices, local(): lax.psum_scatter(score_block(lowered, store), 'col', scatter_dimension=0,...  63 us
    all_gather x2, waiting for transfers between devices, local(): lax.all_gather(local_rows, 'col', axis=0, tiled=True)  53.8 us
    dot_general x2, matrix products, score_block(): lax.dot_general(lowered, store, (((1,), (1,)), ((), ())), preferred_eleme...  25 us
  transfers between devices with their start and end apart: 5, of which 5 were waited for; matrix products, arithmetic and copies ran while one was open for 15% of the time, Pallas kernels for 0%

commit v1 on v0

--- a/solution.py
+++ b/solution.py
@@ -20,7 +20,7 @@
             precision=lax.Precision.HIGHEST,
             preferred_element_type=jnp.float32,
         )
-        summed = lax.psum(partial_rows, "row")
+        summed = jnp.sum(lax.all_gather(partial_rows, "row"), axis=0)
         lowered = (summed * column_gain[None, :]).astype(jnp.bfloat16)
         own_scores = lax.psum_scatter(
             score_block(lowered, store), "col", scatter_dimension=0, tiled=True

time: 336 us -> 357 us (1.062)
  waiting for transfers between devices: 217 us -> 228 us
  other arithmetic: 1.9 us -> 10.2 us
    all_gather x0 -> x2, waiting for transfers between devices: none -> 113 us  [local(): summed = jnp.sum(lax.all_gather(partial_rows, 'row'), axis=0)]
    psum x1 -> x0, waiting for transfers between devices: 99 us -> none  [local(): summed = lax.psum(partial_rows, 'row')]
    reduce_sum x0 -> x2, other arithmetic: none -> 8.34 us  [local(): summed = jnp.sum(lax.all_gather(partial_rows, 'row'), axis=0)]
  transfers between devices with their start and end apart: 5 -> 6, of which waited for: 5 -> 6; matrix products, arithmetic and copies ran while one was open for 15% -> 31% of each run, Pallas kernels for 0% -> 0%
where the time goes in v1:
time: 357 us; the launch traced here: 356 us
  waiting for transfers between devices  228 us (64%)
  matrix products  102 us (29%)
  between operations  13.5 us (4%)
  other arithmetic  10.2 us (3%)
    all_gather x2, waiting for transfers between devices, local(): summed = jnp.sum(lax.all_gather(partial_rows, 'row'), axis=0)  113 us
    dot_general x2, matrix products, local(): jnp.dot(lax.all_gather(local_rows, 'col', axis=0, tiled=True), precond, p...  76.7 us
    reduce_scatter x2, waiting for transfers between devices, local(): lax.psum_scatter(score_block(lowered, store), 'col', scatter_dimension=0,...  60.8 us
    all_gather x2, waiting for transfers between devices, local(): lax.all_gather(local_rows, 'col', axis=0, tiled=True)  53.8 us
    dot_general x2, matrix products, score_block(): lax.dot_general(lowered, store, (((1,), (1,)), ((), ())), preferred_eleme...  25.3 us
    reduce_sum x2, other arithmetic, local(): summed = jnp.sum(lax.all_gather(partial_rows, 'row'), axis=0)  8.34 us
  transfers between devices with their start and end apart: 6, of which 6 were waited for; matrix products, arithmetic and copies ran while one was open for 31% of the time, Pallas kernels for 0%

profile of v1, /device:TPU:0, one launch (start us, length us, event | category | flops | bytes accessed | tf_op | source)
XLA Modules:
  0.0 356.4 jit_solution(12187104062120068040)
XLA Ops:
  6.5 0.0 all-gather.9.cloned.1.call-start
  6.5 2.2 fusion.8
  8.7 0.0 all-gather.9.cloned.1.call-update
  8.7 0.0 all-gather.13.cloned.1.call-start
  8.8 0.7 all-gather.13.cloned.1.call-update
  9.5 0.0 all-gather.11.cloned.1.call-start
  9.5 46.9 %all-gather.9.cloned.1.call-done = f32[1,192,5120]{2,1,0:T(8,128)} async-done(((f32[1,24,5120]{2,1,0:T(8,128)}), f32[1,192,5120]{2,1,0:T(8,128)}) %all-gather.9.cloned.1.call-update) | async-done | bytes 3932176 | tf_op jit(solution)/shard_map/all_gather | solution.py:18
  56.4 38.3 %fusion.2 = f32[192,2560]{1,0:T(8,128)} fusion(f32[5120,2560]{1,0:T(8,128)} %param.5, f32[1,192,5120]{2,1,0:T(8,128)} %all-gather.9.cloned.1.call-done), kind=kOutput, calls=%fused_computation.2 | convolution fusion | flops 30198988800 | bytes 58327040 | tf_op jit(solution)/shard_map/dot_general | solution.py:17
  94.7 0.0 all-gather.11.cloned.1.call-update
  94.8 0.0 all-gather.15.cloned.1.call-start
  94.8 6.9 %all-gather.13.cloned.1.call-done = f32[1,192,5120]{2,1,0:T(8,128)} async-done(((f32[1,24,5120]{2,1,0:T(8,128)}), f32[1,192,5120]{2,1,0:T(8,128)}) %all-gather.13.cloned.1.call-update) | async-done | bytes 3932176 | tf_op jit(solution)/shard_map/all_gather | solution.py:18
  101.7 38.4 %fusion = f32[192,2560]{1,0:T(8,128)} fusion(f32[5120,2560]{1,0:T(8,128)} %param.5, f32[1,192,5120]{2,1,0:T(8,128)} %all-gather.13.cloned.1.call-done), kind=kOutput, calls=%fused_computation | convolution fusion | flops 30198988800 | bytes 58327040 | tf_op jit(solution)/shard_map/dot_general | solution.py:17
  140.1 0.0 all-gather.15.cloned.1.call-update
  140.1 0.0 reduce-scatter.3.cloned.1.call-start
  140.1 45.4 %all-gather.11.cloned.1.call-done = f32[768,2560]{1,0:T(8,128)} async-done(((f32[192,2560]{1,0:T(8,128)}), f32[768,2560]{1,0:T(8,128)}) %all-gather.11.cloned.1.call-update) | async-done | bytes 7864336 | tf_op jit(solution)/shard_map/all_gather | solution.py:23
  185.5 0.0 copy-start
  185.5 4.2 %reduce_sum.18 = f32[192,2560]{1,0:T(8,128)S(1)} reduce(f32[4,192,2560]{2,1,0:T(8,128)} %bitcast.15, f32[]{:T(128)} %constant.0.clone.1), dimensions={0}, to_apply=%region_0.0 | reduce | flops 1474560 | bytes 9830404 | tf_op jit(solution)/shard_map/reduce_sum | solution.py:23
  189.7 0.0 copy-done
  189.7 13.0 %fusion.4 = f32[192,3072]{1,0:T(8,128)} fusion(bf16[3072,2560]{1,0:T(8,128)(2,1)} %param.7, f32[192,2560]{1,0:T(8,128)S(1)} %reduce_sum.18, f32[2560]{0:T(1024)S(1)} %copy-done), kind=kOutput, calls=%fused_computation.6 | convolution fusion | flops 3020881920 | bytes 20064256 | tf_op jit(solution)/shard_map/dot_general | solution.py:8
  202.7 0.0 reduce-scatter.3.cloned.1.call-update
  202.7 0.2 reduce-scatter.5.cloned.1.call-start
  202.9 67.4 %all-gather.15.cloned.1.call-done = f32[768,2560]{1,0:T(8,128)} async-done(((f32[192,2560]{1,0:T(8,128)}), f32[768,2560]{1,0:T(8,128)}) %all-gather.15.cloned.1.call-update) | async-done | bytes 7864336 | tf_op jit(solution)/shard_map/all_gather | solution.py:23
  270.3 4.2 %reduce_sum.19 = f32[192,2560]{1,0:T(8,128)S(1)} reduce(f32[4,192,2560]{2,1,0:T(8,128)} %bitcast.14, f32[]{:T(128)} %constant.0.clone.1), dimensions={0}, to_apply=%region_2.0 | reduce | flops 1474560 | bytes 9830404 | tf_op jit(solution)/shard_map/reduce_sum | solution.py:23
  274.5 12.3 %fusion.5 = f32[192,3072]{1,0:T(8,128)} fusion(bf16[3072,2560]{1,0:T(8,128)(2,1)} %param.7, f32[192,2560]{1,0:T(8,128)S(1)} %reduce_sum.19, f32[2560]{0:T(1024)S(1)} %copy-done), kind=kOutput, calls=%fused_computation.7 | convolution fusion | flops 3020881920 | bytes 20064256 | tf_op jit(solution)/shard_map/dot_general | solution.py:8
  286.9 0.0 reduce-scatter.5.cloned.1.call-update
  286.9 22.7 %reduce-scatter.3.cloned.1.call-done = f32[24,3072]{1,0:T(8,128)} async-done(((f32[192,3072]{1,0:T(8,128)}), f32[24,3072]{1,0:T(8,128)}) %reduce-scatter.3.cloned.1.call-update) | async-done | bytes 294928 | tf_op jit(solution)/shard_map/reduce_scatter | solution.py:25
  309.6 38.1 %reduce-scatter.5.cloned.1.call-done = f32[24,3072]{1,0:T(8,128)} async-done(((f32[192,3072]{1,0:T(8,128)}), f32[24,3072]{1,0:T(8,128)}) %reduce-scatter.5.cloned.1.call-update) | async-done | bytes 294928 | tf_op jit(solution)/shard_map/reduce_scatter | solution.py:25
  347.7 1.9 pad_maximum_fusion
Async XLA Ops:
  6.5 49.9 %all-gather.9.cloned.1.call-start = ((), (), s32[]{:S(2)}) async-start(), calls=%async_computation.4 | async-start | bytes 4423680 | tf_op jit(solution)/shard_map/all_gather | solution.py:18
  8.7 93.0 %all-gather.13.cloned.1.call-start = ((), (), s32[]{:S(2)}) async-start(), calls=%async_computation.6 | async-start | bytes 4423680 | tf_op jit(solution)/shard_map/all_gather | solution.py:18
  9.5 176.0 %all-gather.11.cloned.1.call-start = ((), (), s32[]{:S(2)}) async-start(), calls=%async_computation.5 | async-start | bytes 9830400 | tf_op jit(solution)/shard_map/all_gather | solution.py:23
  94.8 175.6 %all-gather.15.cloned.1.call-start = ((), (), s32[]{:S(2)}) async-start(), calls=%async_computation.7 | async-start | bytes 9830400 | tf_op jit(solution)/shard_map/all_gather | solution.py:23
  140.1 169.5 %reduce-scatter.3.cloned.1.call-start = ((), (), s32[]{:S(2)}) async-start(), calls=%async_computation.2 | async-start | bytes 2654208 | tf_op jit(solution)/shard_map/reduce_scatter | solution.py:25
  185.5 4.2 %copy-start = (f32[2560]{0:T(1024)S(1)}, f32[2560]{0:T(1024)}, u32[]{:S(2)}) copy-start(f32[2560]{0:T(1024)} %param.6) | copy-start | bytes 30724
  202.7 145.0 %reduce-scatter.5.cloned.1.call-start = ((), (), s32[]{:S(2)}) async-start(), calls=%async_computation.3 | async-start | bytes 2654208 | tf_op jit(solution)/shard_map/reduce_scatter | solution.py:25
Sparse Core Ops, SparseCore 0:
  9.0 47.4 all-gather.8
  58.1 43.5 all-gather.12
  103.5 81.8 all-gather.10
  187.2 83.1 all-gather.14
  272.5 37.0 reduce-scatter.2
  311.8 35.8 reduce-scatter.4
